TPU v7x, 512 devices: a whole 4x8x8 slice. The times are simulated.
512 devices in a mesh: wide: 64 (over x, y, core), narrow: 8 (over z).
Axes of the slice: x: 4, y: 8, z: 8, core: 2. Of those that a mesh axis runs over, the one named last changes fastest.
Arguments:
- orbitals: float32 [448, 56, 7, 512], P('wide', 'narrow'), may hold values from -6 to 6
- cell_matrix: bfloat16 [64, 8, 1, 512, 512], P('wide', 'narrow'), as said below
- cell_order: int32 [64, 8, 1, 512], P('wide', 'narrow'), may hold values from 0 to 511, as said below
Outputs:
- filtered_basis: float32 [448, 56, 7, 512], P('wide', 'narrow')
Inputs may be any that keep to these rules, and one draw needn't show every extreme that they name: Each row of cell_order lists the 512 cell node numbers of one cell in the order given by one of the 48 rotations and reflections of the cube. `cell_matrix`: each cell's matrix is symmetric.
All inputs are finite; a program needn't handle non-finite values.
Results may differ from a plain program's by a relative error of at most 0.00045.
The roundings to bfloat16 on the way count: a program that leaves them out, or rounds other values in their place, can miss the bound.
Values sent between devices are 32-bit elements; how exact they have to be, the bound alone decides.
A program may use at most 64 MiB of HBM per device.

v0:
```python
import functools

import jax
import jax.numpy as jnp
from jax import lax
from jax.experimental import pallas as pl
from jax.experimental.pallas import tpu as pltpu
from jax.sharding import PartitionSpec as P

MESH=pl.DeviceIdType.MESH
XS,YS,ZS=4,8,8
TILES=160
HALF=TILES//2
CA=HALF//XS
CB=3

def place():
    w=lax.axis_index("wide"); z=lax.axis_index("narrow")
    x=w//16; y=(w//2)%8; core=w%2
    return x,y,z,core

def at(x,y,z,core):
    return {"wide": x*16+y*2+core, "narrow": z}

def peers(x,y,z,core):
    out=[at(x,y,z,1-core)]
    for d in range(1,XS): out.append(at((x+d)%XS,y,z,core))
    for d in range(1,YS): out.append(at(x,(y+d)%YS,z,core))
    for d in range(1,ZS): out.append(at(x,y,(z+d)%ZS,core))
    return out

def ar_scratch():
    f=jnp.float32
    return [pltpu.VMEM((HALF,8,128),f),
            pltpu.VMEM((HALF,8,128),f),
            pltpu.VMEM((XS,CA,8,128),f),
            pltpu.VMEM((YS*CB,8,128),f),
            pltpu.VMEM((YS,CB,8,128),f),
            pltpu.VMEM((CB,8,128),f),
            pltpu.VMEM((ZS,CB,8,128),f),
            pltpu.VMEM((YS*CB,8,128),f),
            pltpu.SemaphoreType.DMA((40,)),
            pltpu.SemaphoreType.DMA((40,))]

def all_reduce(g, full, rc, acc, rx, sx, ry, sy, rz, gy, ssem, rsem):
    x,y,z,core=place()
    pend=[]
    cnt=[0]
    def send(src,dst,to):
        k=cnt[0]; cnt[0]+=1
        c=pltpu.make_async_remote_copy(src_ref=src,dst_ref=dst,send_sem=ssem.at[k],recv_sem=rsem.at[k],device_id=to,device_id_type=MESH)
        c.start(); pend.append(c)
        return c
    other=1-core
    c=send(g.at[pl.ds(other*HALF,HALF)],rc,at(x,y,z,other))
    c.wait_recv()
    acc[...]=g[pl.ds(core*HALF,HALF)]+rc[...]
    cs=[send(acc.at[pl.ds(((x+d)%XS)*CA,CA)],rx.at[d],at((x+d)%XS,y,z,core)) for d in range(1,XS)]
    for c in cs: c.wait_recv()
    s=acc[pl.ds(x*CA,CA)]
    for d in range(1,XS): s=s+rx[d]
    sx[0:CA]=s
    sx[CA:]=jnp.zeros((YS*CB-CA,8,128),jnp.float32)
    cs=[send(sx.at[pl.ds(((y+d)%YS)*CB,CB)],ry.at[d],at(x,(y+d)%YS,z,core)) for d in range(1,YS)]
    for c in cs: c.wait_recv()
    s=sx[pl.ds(y*CB,CB)]
    for d in range(1,YS): s=s+ry[d]
    sy[...]=s
    cs=[send(sy,rz.at[d],at(x,y,(z+d)%ZS,core)) for d in range(1,ZS)]
    for c in cs: c.wait_recv()
    for d in range(1,ZS): s=s+rz[d]
    gy[pl.ds(y*CB,CB)]=s
    cs=[send(gy.at[pl.ds(y*CB,CB)],gy.at[pl.ds(y*CB,CB)],at(x,(y+d)%YS,z,core)) for d in range(1,YS)]
    for c in cs: c.wait_recv()
    mine=core*HALF+x*CA
    full[pl.ds(mine,CA)]=gy[0:CA]
    cs=[send(gy.at[pl.ds(0,CA)],full.at[pl.ds(mine,CA)],at((x+d)%XS,y,z,core)) for d in range(1,XS)]
    f0=send(gy.at[pl.ds(0,CA)],full.at[pl.ds(mine,CA)],at(x,y,z,other))
    fs=[f0]
    for d in range(1,XS):
        cs[d-1].wait_recv()
        src=core*HALF+((x-d+XS)%XS)*CA
        fs.append(send(full.at[pl.ds(src,CA)],full.at[pl.ds(src,CA)],at(x,y,z,other)))
    for c in fs: c.wait_recv()
    for c in pend: c.wait_send()

def barrier(ps):
    sem=pltpu.get_barrier_semaphore()
    for p in ps: pl.semaphore_signal(sem,inc=1,device_id=p,device_id_type=MESH)
    pl.semaphore_wait(sem,len(ps))


DEG = 4
BAND_LOW = 4.0
BAND_HIGH = 34.0
ANCHOR = 0.0
WIDE, NARROW = XS * YS * 2, ZS
PART = 2
COLS = 512 // PART


def coefficients():
    center = (BAND_LOW + BAND_HIGH) / 2.0
    half = (BAND_HIGH - BAND_LOW) / 2.0
    sigma = half / (ANCHOR - center)
    tau = 2.0 / sigma
    out = [(sigma / half, 0.0)]
    for _ in range(DEG - 1):
        fresh = 1.0 / (tau - sigma)
        out.append((2.0 * fresh / half, sigma * fresh))
        sigma = fresh
    return center, out


def filter_scratch():
    f = jnp.float32
    return [
        pltpu.VMEM((512, 512), jnp.bfloat16),
        pltpu.VMEM((DEG, PART, 8, 8, 8, COLS), f),
        pltpu.VMEM((DEG, PART, 8, 8, 8, COLS), f),
        pltpu.VMEM((DEG, PART, 2, 8, 8, COLS), f),
        pltpu.VMEM((DEG, PART, 2, 8, 8, COLS), f),
        pltpu.VMEM((DEG, PART, 2, 2, 8, COLS), f),
        pltpu.SemaphoreType.DMA((DEG + 1, PART, 8)),
        pltpu.SemaphoreType.DMA((DEG + 1, PART, 8)),
    ]


def filter_steps(orbitals, matrix, order, field, mat, ys, zs, fw, fn, ce, ssem, rsem):
    w = lax.axis_index("wide")
    n = lax.axis_index("narrow")
    wn, wp = (w + 1) % WIDE, (w + WIDE - 1) % WIDE
    nn, np_ = (n + 1) % NARROW, (n + NARROW - 1) % NARROW
    center, weights = coefficients()
    pend = []

    def send(src, dst, r, h, k, to):
        c = pltpu.make_async_remote_copy(
            src_ref=src,
            dst_ref=dst,
            send_sem=ssem.at[r, h, k],
            recv_sem=rsem.at[r, h, k],
            device_id={"wide": to[0], "narrow": to[1]},
            device_id_type=MESH,
        )
        c.start()
        pend.append(c)
        return c

    copies = {}
    for h in range(PART):
        cols = slice(COLS * h, COLS * h + COLS)
        for i in range(7):
            for j in range(7):
                ys[0, h, i, j, 0:7] = orbitals[i, j, :, cols]
                ys[0, h, i, j, 7:8] = orbitals[i, j, 0:1, cols]
        y = ys.at[0, h]
        copies[0, h] = [
            send(y.at[0, 0:7], y.at[7, 0:7], 0, h, 0, (wp, n)),
            send(y.at[0:7, 0], y.at[0:7, 7], 0, h, 1, (w, np_)),
            send(y.at[0, 0], y.at[7, 7], 0, h, 2, (wp, np_)),
        ]
    place_of = jnp.where(
        lax.broadcasted_iota(jnp.int32, (512, 512), 0) == jnp.broadcast_to(order[...], (512, 512)), 1.0, 0.0
    ).astype(jnp.bfloat16)
    rows_placed = jnp.dot(place_of, matrix[...], preferred_element_type=jnp.float32).astype(jnp.bfloat16)
    mat[...] = lax.dot_general(
        rows_placed, place_of, (((1,), (1,)), ((), ())), preferred_element_type=jnp.float32
    ).astype(jnp.bfloat16)

    sub = lax.broadcasted_iota(jnp.int32, (8, 8, COLS), 1)

    def updated(image, r, h, i, j):
        out = (image - center * ys[r, h, i, j]) * weights[r][0]
        if r > 0:
            out = out - weights[r][1] * ys[r - 1, h, i, j]
        return out

    def store(r, h, i, j, value):
        if r < DEG - 1:
            ys[r + 1, h, i, j] = value
        elif not isinstance(i, int) or i < 7:
            field[h, i, j] = value

    def interior(r, h):
        inner = slice(1, 7)
        for i in range(1, 7):
            value = updated(zs[r, h, i, inner], r, h, i, inner)
            if r == DEG - 1:
                value = jnp.where(sub[1:7] < 7, value, 0.0)
            store(r, h, i, inner, value)

    def border(r, h):
        last = r == DEG - 1
        keep = (lambda v: jnp.where(sub[0, :, :] < 7, v, 0.0)) if last else (lambda v: v)
        for i in range(7 if last else 8):
            edge = i in (0, 7)
            for j in range(8) if edge else (0, 7):
                if last and j == 7:
                    field[h, i, 7] = jnp.zeros((8, COLS), jnp.float32)
                    continue
                image = zs[r, h, i, j]
                a, b = (0 if i == 0 else 1), (0 if j == 0 else 1)
                if edge:
                    image = image + fw[r, h, a, j]
                if j in (0, 7):
                    image = image + fn[r, h, b, i]
                    if edge:
                        image = image + ce[r, h, a, b]
                store(r, h, i, j, keep(updated(image, r, h, i, j)))

    for r in range(DEG):
        for h in range(PART):
            for c in copies[r, h]:
                c.wait_recv()
            if r > 0:
                border(r - 1, h)
            rounded = ys[r, h].reshape(512, COLS).astype(jnp.bfloat16)
            product = jnp.dot(mat[...], rounded, preferred_element_type=jnp.float32).reshape(8, 8, 8, COLS)
            for i in range(8):
                v = product[i]
                joined = jnp.where(
                    sub == 0, pltpu.roll(v, 1, axis=1), jnp.where(sub == 7, pltpu.roll(v, 7, axis=1), 0.0)
                )
                zs[r, h, i] = v + joined
            z, gw, gn, gc = zs.at[r, h], fw.at[r, h], fn.at[r, h], ce.at[r, h]
            cs = [
                send(z.at[7], gw.at[0], r + 1, h, 0, (wn, n)),
                send(z.at[:, 7], gn.at[0], r + 1, h, 1, (w, nn)),
                send(z.at[7, 7], gc.at[0, 0], r + 1, h, 2, (wn, nn)),
            ]
            if r < DEG - 1:
                cs += [
                    send(z.at[0], gw.at[1], r + 1, h, 3, (wp, n)),
                    send(z.at[:, 0], gn.at[1], r + 1, h, 4, (w, np_)),
                    send(z.at[7, 0], gc.at[0, 1], r + 1, h, 5, (wn, np_)),
                    send(z.at[0, 7], gc.at[1, 0], r + 1, h, 6, (wp, nn)),
                    send(z.at[0, 0], gc.at[1, 1], r + 1, h, 7, (wp, np_)),
                ]
            copies[r + 1, h] = cs
            interior(r, h)
    for h in range(PART):
        for c in copies[DEG, h]:
            c.wait_recv()
        border(DEG - 1, h)
    return pend


def neighbours(w, n):
    return [
        {"wide": (w + a) % WIDE, "narrow": (n + b) % NARROW}
        for a in (WIDE - 1, 0, 1)
        for b in (NARROW - 1, 0, 1)
        if (a, b) != (0, 0)
    ]


def gram_tiles(field, tiles):
    def dot_tn(a, b):
        return lax.dot_general(
            a, b, (((0,), (0,)), ((), ())), precision=lax.Precision.HIGHEST, preferred_element_type=jnp.float32
        )

    cols = [field[h].reshape(448, COLS) for h in range(PART)]
    per = COLS // 128
    for a in range(PART):
        for b in range(a + 1):
            block = dot_tn(cols[a], cols[b])
            for i in range(per):
                for j in range(per):
                    p, q = a * per + i, b * per + j
                    if q <= p:
                        t = 16 * (p * (p + 1) // 2 + q)
                        tiles[t : t + 16] = block[128 * i : 128 * i + 128, 128 * j : 128 * j + 128].reshape(16, 8, 128)


def filter_kernel(orbitals, matrix, order, field, full, tiles, *scratch):
    barrier(neighbours(lax.axis_index("wide"), lax.axis_index("narrow")) + peers(*place()))
    pend = filter_steps(orbitals, matrix, order, field, *scratch[:8])
    gram_tiles(field, tiles)
    all_reduce(tiles, full, *scratch[8:])
    for c in pend:
        c.wait_send()


def filter_call(orbitals, matrix, order):
    return pl.pallas_call(
        filter_kernel,
        out_shape=(
            jax.ShapeDtypeStruct((PART, 7, 8, 8, COLS), jnp.float32),
            jax.ShapeDtypeStruct((TILES, 8, 128), jnp.float32),
        ),
        in_specs=[pl.BlockSpec(memory_space=pltpu.VMEM)] * 3,
        out_specs=[pl.BlockSpec(memory_space=pltpu.VMEM)] * 2,
        scratch_shapes=[pltpu.VMEM((TILES, 8, 128), jnp.float32)] + filter_scratch() + ar_scratch(),
        compiler_params=pltpu.CompilerParams(collective_id=0, has_side_effects=True, vmem_limit_bytes=48 << 20),
    )(orbitals, matrix, order)


def dot_nn(a, b):
    return lax.dot_general(
        a, b, (((1,), (0,)), ((), ())), precision=lax.Precision.HIGHEST, preferred_element_type=jnp.float32
    )


def dot_nt(a, b):
    return lax.dot_general(
        a, b, (((1,), (1,)), ((), ())), precision=lax.Precision.HIGHEST, preferred_element_type=jnp.float32
    )


def reciprocal(d):
    r = pl.reciprocal(d, approx=True)
    r = r * (2.0 - d * r)
    return r * (2.0 - d * r)


def inverse_factor(block):
    rows = [block[8 * i : 8 * i + 8, :] for i in range(16)]
    lane = lax.broadcasted_iota(jnp.int32, (8, 128), 1)
    sub = lax.broadcasted_iota(jnp.int32, (8, 128), 0)
    for b in range(16):
        first = 8 * b
        panel = [jnp.broadcast_to(rows[b][i : i + 1, :], (8, 128)) for i in range(8)]
        e = {}
        for i in range(8):
            for j in range(i, 8):
                e[i, j] = jnp.broadcast_to(panel[i][:, first + j : first + j + 1], (8, 128))
        inside = (lane >= first) & (lane < first + 8)
        p = [jnp.where(inside, jnp.where(lane == first + i, 1.0, 0.0), panel[i]) for i in range(8)]
        inv = [None] * 8
        m = {}
        for k in range(8):
            inv[k] = reciprocal(e[k, k])
            for i in range(k + 1, 8):
                m[i, k] = e[k, i] * inv[k]
                for j in range(i, 8):
                    e[i, j] = e[i, j] - m[i, k] * e[k, j]
                p[i] = p[i] - m[i, k] * p[k]
        if b < 15:
            s = [p[k] * inv[k] for k in range(8)]
            for l in range(6, -1, -1):
                for k in range(7, l, -1):
                    s[l] = s[l] - m[k, l] * s[k]
            for i in range(b + 1, 16):
                below = rows[i]
                total = jnp.where(inside, 0.0, below)
                for k in range(8):
                    total = total - jnp.broadcast_to(below[:, first + k : first + k + 1], (8, 128)) * s[k]
                rows[i] = total
        own, pivot = p[0], e[0, 0]
        for k in range(1, 8):
            own = jnp.where(sub == k, p[k], own)
            pivot = jnp.where(sub == k, e[k, k], pivot)
        y = lax.rsqrt(pivot)
        y = y * (1.5 - 0.5 * pivot * y * y)
        rows[b] = jnp.where(lane <= sub + first, own, 0.0) * y
    return jnp.concatenate(rows, axis=0)


def finish_kernel(node_total, packed, field, out, w, x, f):
    for i in range(4):
        for j in range(i + 1):
            at_tile = 16 * (i * (i + 1) // 2 + j)
            w[128 * i : 128 * i + 128, 128 * j : 128 * j + 128] = (
                packed[at_tile : at_tile + 16].reshape(128, 128) * (1.0 / node_total)
            )
    for h in range(PART):
        f[:, COLS * h : COLS * h + COLS] = field[h].reshape(448, COLS)
    lower = {}
    for j in range(4):
        here = slice(128 * j, 128 * j + 128)
        inverse = inverse_factor(w[here, here])
        if j < 3:
            column = dot_nt(w[128 * (j + 1) :, here], inverse)
            lower[j] = column
            for i in range(j + 1, 4):
                band = column[128 * (i - j - 1) : 128 * (i - j)]
                w[128 * i : 128 * i + 128, 128 * (j + 1) : 128 * (i + 1)] = w[
                    128 * i : 128 * i + 128, 128 * (j + 1) : 128 * (i + 1)
                ] - dot_nt(band, column[: 128 * (i - j)])
        x[here, here] = inverse
        if j > 0:
            left = jnp.concatenate([lower[k][128 * (j - k - 1) : 128 * (j - k)] for k in range(j)], axis=1)
            x[here, : 128 * j] = -dot_nn(inverse, dot_nn(left, x[: 128 * j, : 128 * j]))
        product = dot_nt(f[:, : 128 * (j + 1)], x[here, : 128 * (j + 1)])
        for a in range(7):
            for b in range(7):
                r = 64 * a + 8 * b
                out[a, b, :, here] = product[r : r + 7, :]
        if j < 3:
            x[here, 128 * (j + 1) :] = jnp.zeros((128, 512 - 128 * (j + 1)), jnp.float32)


def finish_call(packed, field, node_total):
    return pl.pallas_call(
        functools.partial(finish_kernel, node_total),
        out_shape=jax.ShapeDtypeStruct((7, 7, 7, 512), jnp.float32),
        in_specs=[pl.BlockSpec(memory_space=pltpu.VMEM)] * 2,
        out_specs=pl.BlockSpec(memory_space=pltpu.VMEM),
        scratch_shapes=[
            pltpu.VMEM((512, 512), jnp.float32),
            pltpu.VMEM((512, 512), jnp.float32),
            pltpu.VMEM((448, 512), jnp.float32),
        ],
        compiler_params=pltpu.CompilerParams(vmem_limit_bytes=40 << 20),
    )(packed, field)


def on_device(orbitals, cell_matrix, cell_order):
    node_total = 343.0 * WIDE * NARROW
    field, total = filter_call(orbitals, cell_matrix.reshape(512, 512), cell_order.reshape(1, 512))
    return finish_call(total, field, node_total)


def solution(mesh):
    return jax.shard_map(
        on_device,
        mesh=mesh,
        in_specs=(
            P("wide", "narrow", None, None),
            P("wide", "narrow", None, None, None),
            P("wide", "narrow", None, None),
        ),
        out_specs=P("wide", "narrow", None, None),
        check_vma=False,
    )
```

profile of v0, /device:TPU:1, one launch (start us, length us, event | category | flops | bytes accessed | tf_op | source)
XLA Modules:
  0.0 108.1 jit_solution(12271387673249412760)
XLA Ops:
  0.0 0.0 copy-start.2
  0.0 0.7 copy-done.2
  0.7 0.0 copy-start
  0.7 1.1 %copy-done = f32[7,7,7,512]{3,2,1,0:T(8,128)S(1)} copy-done((f32[7,7,7,512]{3,2,1,0:T(8,128)S(1)}, f32[7,7,7,512]{3,2,1,0:T(8,128)}, u32[]{:S(2)}) %copy-start) | copy-done | bytes 702488
  1.8 0.0 copy-start.1
  1.8 1.0 copy-done.1
  2.9 77.6 %shard_map.37 = (f32[2,7,8,8,256]{4,3,2,1,0:T(8,128)S(1)}, f32[160,8,128]{2,1,0:T(8,128)S(1)}) custom-call(f32[7,7,7,512]{3,2,1,0:T(8,128)S(1)} %copy-done, bf16[512,512]{1,0:T(8,128)(2,1)S(1)} %bitcast.2, s32[1,512]{1,0:T(1,128)S(1)} %bitcast.3), custom_call_target="tpu_custom_call" | custom-call | tf_op jit(solution)/shard_map/pallas_call | solution.py:287
  80.5 27.7 %shard_map.38 = f32[7,7,7,512]{3,2,1,0:T(8,128)} custom-call(f32[160,8,128]{2,1,0:T(8,128)S(1)} %get-tuple-element.7.packed, f32[2,7,8,8,256]{4,3,2,1,0:T(8,128)S(1)} %get-tuple-element.8.field), custom_call_target="tpu_custom_call" | custom-call | tf_op jit(solution)/shard_map/pallas_call | solution.py:396
Async XLA Ops:
  0.0 0.7 copy-start.2
  0.7 1.1 %copy-start = (f32[7,7,7,512]{3,2,1,0:T(8,128)S(1)}, f32[7,7,7,512]{3,2,1,0:T(8,128)}, u32[]{:S(2)}) copy-start(f32[7,7,7,512]{3,2,1,0:T(8,128)} %orbitals.1) | copy-start | bytes 2107396
  1.8 1.0 copy-start.1
where the time goes:
time: 108 us
  Pallas kernels  105 us (97%)
  local copies, waits for them, and re-layouts  2.86 us (3%)
    pallas_call x1, Pallas kernels, filter_call(): pl.pallas_call(filter_kernel, out_shape=(jax.ShapeDtypeStruct((PART, 7, 8...  77.6 us
    pallas_call x1, Pallas kernels, finish_call(): pl.pallas_call(functools.partial(finish_kernel, node_total), out_shape=ja...  27.7 us
    unnamed x6, local copies, waits for them, and re-layouts  2.86 us

commit v1 on v0

--- a/solution.py
+++ b/solution.py
@@ -126,7 +126,7 @@
     ]
 
 
-def filter_steps(orbitals, matrix, order, field, mat, ys, zs, fw, fn, ce, ssem, rsem):
+def filter_steps(loads, matrix, order, field, mat, ys, zs, fw, fn, ce, ssem, rsem):
     w = lax.axis_index("wide")
     n = lax.axis_index("narrow")
     wn, wp = (w + 1) % WIDE, (w + WIDE - 1) % WIDE
@@ -149,17 +149,17 @@
 
     copies = {}
     for h in range(PART):
-        cols = slice(COLS * h, COLS * h + COLS)
+        loads[1 + h].wait()
         for i in range(7):
             for j in range(7):
-                ys[0, h, i, j, 0:7] = orbitals[i, j, :, cols]
-                ys[0, h, i, j, 7:8] = orbitals[i, j, 0:1, cols]
+                ys[0, h, i, j, 7:8] = ys[0, h, i, j, 0:1]
         y = ys.at[0, h]
         copies[0, h] = [
+            send(y.at[0, 0], y.at[7, 7], 0, h, 2, (wp, np_)),
+            send(y.at[0:7, 0], y.at[0:7, 7], 0, h, 1, (w, np_)),
             send(y.at[0, 0:7], y.at[7, 0:7], 0, h, 0, (wp, n)),
-            send(y.at[0:7, 0], y.at[0:7, 7], 0, h, 1, (w, np_)),
-            send(y.at[0, 0], y.at[7, 7], 0, h, 2, (wp, np_)),
         ]
+    loads[0].wait()
     place_of = jnp.where(
         lax.broadcasted_iota(jnp.int32, (512, 512), 0) == jnp.broadcast_to(order[...], (512, 512)), 1.0, 0.0
     ).astype(jnp.bfloat16)
@@ -224,19 +224,20 @@
                 )
                 zs[r, h, i] = v + joined
             z, gw, gn, gc = zs.at[r, h], fw.at[r, h], fn.at[r, h], ce.at[r, h]
-            cs = [
-                send(z.at[7], gw.at[0], r + 1, h, 0, (wn, n)),
-                send(z.at[:, 7], gn.at[0], r + 1, h, 1, (w, nn)),
-                send(z.at[7, 7], gc.at[0, 0], r + 1, h, 2, (wn, nn)),
-            ]
-            if r < DEG - 1:
+            both = r < DEG - 1
+            cs = [send(z.at[7, 7], gc.at[0, 0], r + 1, h, 2, (wn, nn))]
+            if both:
                 cs += [
-                    send(z.at[0], gw.at[1], r + 1, h, 3, (wp, n)),
-                    send(z.at[:, 0], gn.at[1], r + 1, h, 4, (w, np_)),
+                    send(z.at[0, 0], gc.at[1, 1], r + 1, h, 7, (wp, np_)),
                     send(z.at[7, 0], gc.at[0, 1], r + 1, h, 5, (wn, np_)),
                     send(z.at[0, 7], gc.at[1, 0], r + 1, h, 6, (wp, nn)),
-                    send(z.at[0, 0], gc.at[1, 1], r + 1, h, 7, (wp, np_)),
                 ]
+            cs.append(send(z.at[:, 7], gn.at[0], r + 1, h, 1, (w, nn)))
+            if both:
+                cs.append(send(z.at[:, 0], gn.at[1], r + 1, h, 4, (w, np_)))
+            cs.append(send(z.at[7], gw.at[0], r + 1, h, 0, (wn, n)))
+            if both:
+                cs.append(send(z.at[0], gw.at[1], r + 1, h, 3, (wp, n)))
             copies[r + 1, h] = cs
             interior(r, h)
     for h in range(PART):
@@ -274,9 +275,18 @@
                         tiles[t : t + 16] = block[128 * i : 128 * i + 128, 128 * j : 128 * j + 128].reshape(16, 8, 128)
 
 
-def filter_kernel(orbitals, matrix, order, field, full, tiles, *scratch):
+def filter_kernel(orbitals, matrix, order, field, full, tiles, held, lsem, *scratch):
+    ys = scratch[1]
+    loads = [pltpu.make_async_copy(matrix, held, lsem.at[0])] + [
+        pltpu.make_async_copy(
+            orbitals.at[:, :, :, COLS * h : COLS * h + COLS], ys.at[0, h, 0:7, 0:7, 0:7], lsem.at[1 + h]
+        )
+        for h in range(PART)
+    ]
+    for c in loads[1:] + loads[:1]:
+        c.start()
     barrier(neighbours(lax.axis_index("wide"), lax.axis_index("narrow")) + peers(*place()))
-    pend = filter_steps(orbitals, matrix, order, field, *scratch[:8])
+    pend = filter_steps(loads, held, order, field, *scratch[:8])
     gram_tiles(field, tiles)
     all_reduce(tiles, full, *scratch[8:])
     for c in pend:
@@ -290,29 +300,56 @@
             jax.ShapeDtypeStruct((PART, 7, 8, 8, COLS), jnp.float32),
             jax.ShapeDtypeStruct((TILES, 8, 128), jnp.float32),
         ),
-        in_specs=[pl.BlockSpec(memory_space=pltpu.VMEM)] * 3,
+        in_specs=[pl.BlockSpec(memory_space=pl.ANY)] * 2 + [pl.BlockSpec(memory_space=pltpu.VMEM)],
         out_specs=[pl.BlockSpec(memory_space=pltpu.VMEM)] * 2,
-        scratch_shapes=[pltpu.VMEM((TILES, 8, 128), jnp.float32)] + filter_scratch() + ar_scratch(),
+        scratch_shapes=[
+            pltpu.VMEM((TILES, 8, 128), jnp.float32),
+            pltpu.VMEM((512, 512), jnp.bfloat16),
+            pltpu.SemaphoreType.DMA((1 + PART,)),
+        ] + filter_scratch() + ar_scratch(),
         compiler_params=pltpu.CompilerParams(collective_id=0, has_side_effects=True, vmem_limit_bytes=48 << 20),
     )(orbitals, matrix, order)
 
 
+def halves(a):
+    high = a.astype(jnp.bfloat16)
+    return high, (a - high.astype(jnp.float32)).astype(jnp.bfloat16)
+
+
+def product(a, b, dims):
+    (ah, al), (bh, bl) = halves(a), halves(b)
+
+    def one(p, q):
+        return lax.dot_general(p, q, (dims, ((), ())), preferred_element_type=jnp.float32)
+
+    return one(ah, bh) + (one(ah, bl) + one(al, bh))
+
+
 def dot_nn(a, b):
-    return lax.dot_general(
-        a, b, (((1,), (0,)), ((), ())), precision=lax.Precision.HIGHEST, preferred_element_type=jnp.float32
-    )
+    return product(a, b, ((1,), (0,)))
 
 
 def dot_nt(a, b):
-    return lax.dot_general(
-        a, b, (((1,), (1,)), ((), ())), precision=lax.Precision.HIGHEST, preferred_element_type=jnp.float32
-    )
+    return product(a, b, ((1,), (1,)))
 
 
 def reciprocal(d):
     r = pl.reciprocal(d, approx=True)
-    r = r * (2.0 - d * r)
     return r * (2.0 - d * r)
+
+
+def thirds(a):
+    high = a.astype(jnp.bfloat16).astype(jnp.float32)
+    rest = a - high
+    middle = rest.astype(jnp.bfloat16).astype(jnp.float32)
+    return high, middle, rest - middle
+
+
+def outer(r, s):
+    (rh, rm, rl), (sh, sm, sl) = thirds(r), thirds(s)
+    left = jnp.concatenate([rh, rh, rm, rm, rh, rl], axis=0).astype(jnp.bfloat16)
+    right = jnp.concatenate([sh, sm, sh, sm, sl, sh], axis=0).astype(jnp.bfloat16)
+    return lax.dot_general(left, right, (((0,), (0,)), ((), ())), preferred_element_type=jnp.float32)
 
 
 def inverse_factor(block):
@@ -328,30 +365,47 @@
                 e[i, j] = jnp.broadcast_to(panel[i][:, first + j : first + j + 1], (8, 128))
         inside = (lane >= first) & (lane < first + 8)
         p = [jnp.where(inside, jnp.where(lane == first + i, 1.0, 0.0), panel[i]) for i in range(8)]
+        if b < 15:
+            below = rows[b + 1]
+            c = [jnp.broadcast_to(below[:, first + k : first + k + 1], (8, 128)) for k in range(8)]
         inv = [None] * 8
         m = {}
-        for k in range(8):
-            inv[k] = reciprocal(e[k, k])
-            for i in range(k + 1, 8):
-                m[i, k] = e[k, i] * inv[k]
+        for k in range(0, 8, 2):
+            u, v, t = e[k, k], e[k, k + 1], e[k + 1, k + 1]
+            det = u * t - v * v
+            over = reciprocal(det)
+            iu, iv, it = t * over, v * over, u * over
+            inv[k] = reciprocal(u)
+            inv[k + 1] = it
+            m[k + 1, k] = v * inv[k]
+            e[k + 1, k + 1] = det * inv[k]
+            for i in range(k + 2, 8):
+                f, g = e[k, i], e[k + 1, i]
+                one, two = f * iu - g * iv, g * it - f * iv
                 for j in range(i, 8):
-                    e[i, j] = e[i, j] - m[i, k] * e[k, j]
-                p[i] = p[i] - m[i, k] * p[k]
+                    e[i, j] = e[i, j] - (one * e[k, j] + two * e[k + 1, j])
+                m[i, k], m[i, k + 1] = f * inv[k], two
+            p[k + 1] = p[k + 1] - m[k + 1, k] * p[k]
+            for i in range(k + 2, 8):
+                p[i] = p[i] - (m[i, k] * p[k] + m[i, k + 1] * p[k + 1])
+        own, pivot = p[0], e[0, 0]
+        for k in range(1, 8):
+            own = jnp.where(sub == k, p[k], own)
+            pivot = jnp.where(sub == k, e[k, k], pivot)
         if b < 15:
             s = [p[k] * inv[k] for k in range(8)]
             for l in range(6, -1, -1):
                 for k in range(7, l, -1):
                     s[l] = s[l] - m[k, l] * s[k]
-            for i in range(b + 1, 16):
-                below = rows[i]
-                total = jnp.where(inside, 0.0, below)
-                for k in range(8):
-                    total = total - jnp.broadcast_to(below[:, first + k : first + k + 1], (8, 128)) * s[k]
-                rows[i] = total
-        own, pivot = p[0], e[0, 0]
-        for k in range(1, 8):
-            own = jnp.where(sub == k, p[k], own)
-            pivot = jnp.where(sub == k, e[k, k], pivot)
+            terms = [c[k] * s[k] for k in range(8)]
+            while len(terms) > 1:
+                terms = [terms[i] + terms[i + 1] for i in range(0, len(terms), 2)]
+            fresh = jnp.where(inside, 0.0, below) - terms[0]
+            if b < 14:
+                change = outer(own, own * reciprocal(pivot))
+                for i in range(b + 2, 16):
+                    rows[i] = jnp.where(inside, 0.0, rows[i]) - change[8 * i : 8 * i + 8]
+            rows[b + 1] = fresh
         y = lax.rsqrt(pivot)
         y = y * (1.5 - 0.5 * pivot * y * y)
         rows[b] = jnp.where(lane <= sub + first, own, 0.0) * y
@@ -359,14 +413,25 @@
 
 
 def finish_kernel(node_total, packed, field, out, w, x, f):
+    on_diagonal = lax.broadcasted_iota(jnp.int32, (128, 128), 0) == lax.broadcasted_iota(jnp.int32, (128, 128), 1)
+
+    def block(i, j):
+        at_tile = 16 * (i * (i + 1) // 2 + j)
+        return packed[at_tile : at_tile + 16].reshape(128, 128) * (1.0 / node_total)
+
+    scale_row, scale_column = [], []
+    for i in range(4):
+        diagonal = jnp.where(on_diagonal, block(i, i), 0.0)
+        s = jnp.broadcast_to(lax.rsqrt(jnp.sum(diagonal, axis=0, keepdims=True)), (128, 128))
+        scale_row.append(s)
+        scale_column.append(jnp.broadcast_to(jnp.sum(jnp.where(on_diagonal, s, 0.0), axis=1, keepdims=True), (128, 128)))
     for i in range(4):
         for j in range(i + 1):
-            at_tile = 16 * (i * (i + 1) // 2 + j)
-            w[128 * i : 128 * i + 128, 128 * j : 128 * j + 128] = (
-                packed[at_tile : at_tile + 16].reshape(128, 128) * (1.0 / node_total)
-            )
-    for h in range(PART):
-        f[:, COLS * h : COLS * h + COLS] = field[h].reshape(448, COLS)
+            w[128 * i : 128 * i + 128, 128 * j : 128 * j + 128] = block(i, j) * scale_column[i] * scale_row[j]
+    for j in range(4):
+        h, q = divmod(128 * j, COLS)
+        cols = field[h].reshape(448, COLS)[:, q : q + 128]
+        f[:, 128 * j : 128 * j + 128] = cols * scale_row[j][0:1, :]
     lower = {}
     for j in range(4):
         here = slice(128 * j, 128 * j + 128)
@@ -383,11 +448,11 @@
         if j > 0:
             left = jnp.concatenate([lower[k][128 * (j - k - 1) : 128 * (j - k)] for k in range(j)], axis=1)
             x[here, : 128 * j] = -dot_nn(inverse, dot_nn(left, x[: 128 * j, : 128 * j]))
-        product = dot_nt(f[:, : 128 * (j + 1)], x[here, : 128 * (j + 1)])
+        rotated = dot_nt(f[:, : 128 * (j + 1)], x[here, : 128 * (j + 1)])
         for a in range(7):
             for b in range(7):
                 r = 64 * a + 8 * b
-                out[a, b, :, here] = product[r : r + 7, :]
+                out[a, b, :, here] = rotated[r : r + 7, :]
         if j < 3:
             x[here, 128 * (j + 1) :] = jnp.zeros((128, 512 - 128 * (j + 1)), jnp.float32)
 

time: 108 us -> 97.5 us (0.903)
  Pallas kernels: 105 us -> 94.4 us
    pallas_call x1, Pallas kernels: 27.7 us -> 19.5 us  [finish_call(): pl.pallas_call(functools.partial(finish_kernel, node_total), out_shape=ja...]
    pallas_call x1, Pallas kernels: 77.6 us -> 74.8 us  [filter_call(): pl.pallas_call(filter_kernel, out_shape=(jax.ShapeDtypeStruct((PART, 7, 8...]
where the time goes in v1:
time: 97.5 us; the launch traced here: 97.3 us
  Pallas kernels  94.4 us (97%)
  local copies, waits for them, and re-layouts  2.86 us (3%)
    pallas_call x1, Pallas kernels, filter_call(): pl.pallas_call(filter_kernel, out_shape=(jax.ShapeDtypeStruct((PART, 7, 8...  74.8 us
    pallas_call x1, Pallas kernels, finish_call(): pl.pallas_call(functools.partial(finish_kernel, node_total), out_shape=ja...  19.5 us
    unnamed x6, local copies, waits for them, and re-layouts  2.86 us

profile of v1, /device:TPU:1, one launch (start us, length us, event | category | flops | bytes accessed | tf_op | source)
XLA Modules:
  0.0 97.3 jit_solution(6860968400366278060)
XLA Ops:
  0.0 0.0 copy-start.2
  0.0 0.7 copy-done.2
  0.7 0.0 copy-start
  0.7 1.1 %copy-done = f32[7,7,7,512]{3,2,1,0:T(8,128)S(1)} copy-done((f32[7,7,7,512]{3,2,1,0:T(8,128)S(1)}, f32[7,7,7,512]{3,2,1,0:T(8,128)}, u32[]{:S(2)}) %copy-start) | copy-done | bytes 702488
  1.8 0.0 copy-start.1
  1.8 1.0 %copy-done.1 = bf16[1,1,1,512,512]{4,3,2,1,0:T(8,128)(2,1)S(1)} copy-done((bf16[1,1,1,512,512]{4,3,2,1,0:T(8,128)(2,1)S(1)}, bf16[1,1,1,512,512]{4,3,2,1,0:T(8,128)(2,1)}, u32[]{:S(2)}) %copy-start.1) | copy-done | bytes 524312
  2.9 74.8 %shard_map.37 = (f32[2,7,8,8,256]{4,3,2,1,0:T(8,128)S(1)}, f32[160,8,128]{2,1,0:T(8,128)S(1)}) custom-call(f32[7,7,7,512]{3,2,1,0:T(8,128)S(1)} %copy-done, bf16[512,512]{1,0:T(8,128)(2,1)S(1)} %bitcast.2, s32[1,512]{1,0:T(1,128)S(1)} %bitcast.3), custom_call_target="tpu_custom_call" | custom-call | tf_op jit(solution)/shard_map/pallas_call | solution.py:297
  77.7 19.5 %shard_map.38 = f32[7,7,7,512]{3,2,1,0:T(8,128)} custom-call(f32[160,8,128]{2,1,0:T(8,128)S(1)} %get-tuple-element.7.packed, f32[2,7,8,8,256]{4,3,2,1,0:T(8,128)S(1)} %get-tuple-element.8.field), custom_call_target="tpu_custom_call" | custom-call | tf_op jit(solution)/shard_map/pallas_call | solution.py:461
Async XLA Ops:
  0.0 0.7 copy-start.2
  0.7 1.1 %copy-start = (f32[7,7,7,512]{3,2,1,0:T(8,128)S(1)}, f32[7,7,7,512]{3,2,1,0:T(8,128)}, u32[]{:S(2)}) copy-start(f32[7,7,7,512]{3,2,1,0:T(8,128)} %orbitals.1) | copy-start | bytes 2107396
  1.8 1.0 %copy-start.1 = (bf16[1,1,1,512,512]{4,3,2,1,0:T(8,128)(2,1)S(1)}, bf16[1,1,1,512,512]{4,3,2,1,0:T(8,128)(2,1)}, u32[]{:S(2)}) copy-start(bf16[1,1,1,512,512]{4,3,2,1,0:T(8,128)(2,1)} %param.4) | copy-start | bytes 1572868

commit v2 on v1

--- a/solution.py
+++ b/solution.py
@@ -13,6 +13,10 @@
 HALF=TILES//2
 CA=HALF//XS
 CB=3
+
+
+def far_first(count):
+    return sorted(range(1,count),key=lambda d:-min(d,count-d))
 
 def place():
     w=lax.axis_index("wide"); z=lax.axis_index("narrow")
@@ -55,30 +59,30 @@
     c=send(g.at[pl.ds(other*HALF,HALF)],rc,at(x,y,z,other))
     c.wait_recv()
     acc[...]=g[pl.ds(core*HALF,HALF)]+rc[...]
-    cs=[send(acc.at[pl.ds(((x+d)%XS)*CA,CA)],rx.at[d],at((x+d)%XS,y,z,core)) for d in range(1,XS)]
+    cs=[send(acc.at[pl.ds(((x+d)%XS)*CA,CA)],rx.at[d],at((x+d)%XS,y,z,core)) for d in far_first(XS)]
     for c in cs: c.wait_recv()
     s=acc[pl.ds(x*CA,CA)]
     for d in range(1,XS): s=s+rx[d]
     sx[0:CA]=s
     sx[CA:]=jnp.zeros((YS*CB-CA,8,128),jnp.float32)
-    cs=[send(sx.at[pl.ds(((y+d)%YS)*CB,CB)],ry.at[d],at(x,(y+d)%YS,z,core)) for d in range(1,YS)]
+    cs=[send(sx.at[pl.ds(((y+d)%YS)*CB,CB)],ry.at[d],at(x,(y+d)%YS,z,core)) for d in far_first(YS)]
     for c in cs: c.wait_recv()
     s=sx[pl.ds(y*CB,CB)]
     for d in range(1,YS): s=s+ry[d]
     sy[...]=s
-    cs=[send(sy,rz.at[d],at(x,y,(z+d)%ZS,core)) for d in range(1,ZS)]
+    cs=[send(sy,rz.at[d],at(x,y,(z+d)%ZS,core)) for d in far_first(ZS)]
     for c in cs: c.wait_recv()
     for d in range(1,ZS): s=s+rz[d]
     gy[pl.ds(y*CB,CB)]=s
-    cs=[send(gy.at[pl.ds(y*CB,CB)],gy.at[pl.ds(y*CB,CB)],at(x,(y+d)%YS,z,core)) for d in range(1,YS)]
+    cs=[send(gy.at[pl.ds(y*CB,CB)],gy.at[pl.ds(y*CB,CB)],at(x,(y+d)%YS,z,core)) for d in far_first(YS)]
     for c in cs: c.wait_recv()
     mine=core*HALF+x*CA
     full[pl.ds(mine,CA)]=gy[0:CA]
-    cs=[send(gy.at[pl.ds(0,CA)],full.at[pl.ds(mine,CA)],at((x+d)%XS,y,z,core)) for d in range(1,XS)]
+    cs={d: send(gy.at[pl.ds(0,CA)],full.at[pl.ds(mine,CA)],at((x+d)%XS,y,z,core)) for d in far_first(XS)}
     f0=send(gy.at[pl.ds(0,CA)],full.at[pl.ds(mine,CA)],at(x,y,z,other))
     fs=[f0]
-    for d in range(1,XS):
-        cs[d-1].wait_recv()
+    for d in (1,3,2):
+        cs[d].wait_recv()
         src=core*HALF+((x-d+XS)%XS)*CA
         fs.append(send(full.at[pl.ds(src,CA)],full.at[pl.ds(src,CA)],at(x,y,z,other)))
     for c in fs: c.wait_recv()
@@ -160,6 +164,7 @@
             send(y.at[0, 0:7], y.at[7, 0:7], 0, h, 0, (wp, n)),
         ]
     loads[0].wait()
+    loads[1 + PART].wait()
     place_of = jnp.where(
         lax.broadcasted_iota(jnp.int32, (512, 512), 0) == jnp.broadcast_to(order[...], (512, 512)), 1.0, 0.0
     ).astype(jnp.bfloat16)
@@ -275,7 +280,7 @@
                         tiles[t : t + 16] = block[128 * i : 128 * i + 128, 128 * j : 128 * j + 128].reshape(16, 8, 128)
 
 
-def filter_kernel(orbitals, matrix, order, field, full, tiles, held, lsem, *scratch):
+def filter_kernel(orbitals, matrix, order, field, full, tiles, held, numbers, lsem, *scratch):
     ys = scratch[1]
     loads = [pltpu.make_async_copy(matrix, held, lsem.at[0])] + [
         pltpu.make_async_copy(
@@ -283,10 +288,11 @@
         )
         for h in range(PART)
     ]
+    loads.append(pltpu.make_async_copy(order, numbers, lsem.at[1 + PART]))
     for c in loads[1:] + loads[:1]:
         c.start()
     barrier(neighbours(lax.axis_index("wide"), lax.axis_index("narrow")) + peers(*place()))
-    pend = filter_steps(loads, held, order, field, *scratch[:8])
+    pend = filter_steps(loads, held, numbers, field, *scratch[:8])
     gram_tiles(field, tiles)
     all_reduce(tiles, full, *scratch[8:])
     for c in pend:
@@ -300,15 +306,16 @@
             jax.ShapeDtypeStruct((PART, 7, 8, 8, COLS), jnp.float32),
             jax.ShapeDtypeStruct((TILES, 8, 128), jnp.float32),
         ),
-        in_specs=[pl.BlockSpec(memory_space=pl.ANY)] * 2 + [pl.BlockSpec(memory_space=pltpu.VMEM)],
+        in_specs=[pl.BlockSpec(memory_space=pltpu.HBM)] * 3,
         out_specs=[pl.BlockSpec(memory_space=pltpu.VMEM)] * 2,
         scratch_shapes=[
             pltpu.VMEM((TILES, 8, 128), jnp.float32),
             pltpu.VMEM((512, 512), jnp.bfloat16),
-            pltpu.SemaphoreType.DMA((1 + PART,)),
+            pltpu.VMEM((1, 512), jnp.int32),
+            pltpu.SemaphoreType.DMA((2 + PART,)),
         ] + filter_scratch() + ar_scratch(),
         compiler_params=pltpu.CompilerParams(collective_id=0, has_side_effects=True, vmem_limit_bytes=48 << 20),
-    )(orbitals, matrix, order)
+    )(*(pltpu.with_memory_space_constraint(a, pltpu.HBM) for a in (orbitals, matrix, order)))
 
 
 def halves(a):

time: 97.5 us -> 91.7 us (0.941)
  local copies, waits for them, and re-layouts: 2.86 us -> 0 us
  Pallas kernels: 94.4 us -> 91.6 us
    unnamed x6 -> x0, local copies, waits for them, and re-layouts: 2.86 us -> none
    pallas_call x1, Pallas kernels: 74.8 us -> 72 us  [filter_call(): pl.pallas_call(filter_kernel, out_shape=(jax.ShapeDtypeStruct((PART, 7, 8...]
where the time goes in v2:
time: 91.7 us; the launch traced here: 91.6 us
  Pallas kernels  91.6 us (100%)
    pallas_call x1, Pallas kernels, filter_call(): pl.pallas_call(filter_kernel, out_shape=(jax.ShapeDtypeStruct((PART, 7, 8...  72 us
    pallas_call x1, Pallas kernels, finish_call(): pl.pallas_call(functools.partial(finish_kernel, node_total), out_shape=ja...  19.6 us

profile of v2, /device:TPU:1, one launch (start us, length us, event | category | flops | bytes accessed | tf_op | source)
XLA Modules:
  0.0 91.6 jit_solution(9588574150863718329)
XLA Ops:
  0.0 72.0 %shard_map.37 = (f32[2,7,8,8,256]{4,3,2,1,0:T(8,128)S(1)}, f32[160,8,128]{2,1,0:T(8,128)S(1)}) custom-call(f32[7,7,7,512]{3,2,1,0:T(8,128)} %orbitals.1, bf16[512,512]{1,0:T(8,128)(2,1)} %bitcast.2, s32[1,512]{1,0:T(1,128)} %bitcast.3), custom_call_target="tpu_custom_call" | custom-call | tf_op jit(solution)/shard_map/pallas_call | solution.py:303
  72.0 19.6 %shard_map.38 = f32[7,7,7,512]{3,2,1,0:T(8,128)} custom-call(f32[160,8,128]{2,1,0:T(8,128)S(1)} %get-tuple-element.7.packed, f32[2,7,8,8,256]{4,3,2,1,0:T(8,128)S(1)} %get-tuple-element.8.field), custom_call_target="tpu_custom_call" | custom-call | tf_op jit(solution)/shard_map/pallas_call | solution.py:468

commit v3 on v2

--- a/solution.py
+++ b/solution.py
@@ -261,17 +261,22 @@
     ]
 
 
+def halves(a):
+    high = a.astype(jnp.bfloat16)
+    return high, (a - high.astype(jnp.float32)).astype(jnp.bfloat16)
+
+
+def dot_tn(a, b):
+    return lax.dot_general(a, b, (((0,), (0,)), ((), ())), preferred_element_type=jnp.float32)
+
+
 def gram_tiles(field, tiles):
-    def dot_tn(a, b):
-        return lax.dot_general(
-            a, b, (((0,), (0,)), ((), ())), precision=lax.Precision.HIGHEST, preferred_element_type=jnp.float32
-        )
-
-    cols = [field[h].reshape(448, COLS) for h in range(PART)]
+    cols = [halves(field[h].reshape(448, COLS)) for h in range(PART)]
     per = COLS // 128
     for a in range(PART):
         for b in range(a + 1):
-            block = dot_tn(cols[a], cols[b])
+            (ah, al), (bh, bl) = cols[a], cols[b]
+            block = dot_tn(ah, bh) + (dot_tn(ah, bl) + dot_tn(al, bh))
             for i in range(per):
                 for j in range(per):
                     p, q = a * per + i, b * per + j
@@ -318,11 +323,6 @@
     )(*(pltpu.with_memory_space_constraint(a, pltpu.HBM) for a in (orbitals, matrix, order)))
 
 
-def halves(a):
-    high = a.astype(jnp.bfloat16)
-    return high, (a - high.astype(jnp.float32)).astype(jnp.bfloat16)
-
-
 def product(a, b, dims):
     (ah, al), (bh, bl) = halves(a), halves(b)
 
@@ -330,10 +330,6 @@
         return lax.dot_general(p, q, (dims, ((), ())), preferred_element_type=jnp.float32)
 
     return one(ah, bh) + (one(ah, bl) + one(al, bh))
-
-
-def dot_nn(a, b):
-    return product(a, b, ((1,), (0,)))
 
 
 def dot_nt(a, b):
@@ -419,7 +415,7 @@
     return jnp.concatenate(rows, axis=0)
 
 
-def finish_kernel(node_total, packed, field, out, w, x, f):
+def finish_kernel(node_total, packed, field, out, w, f, held, sems):
     on_diagonal = lax.broadcasted_iota(jnp.int32, (128, 128), 0) == lax.broadcasted_iota(jnp.int32, (128, 128), 1)
 
     def block(i, j):
@@ -439,29 +435,27 @@
         h, q = divmod(128 * j, COLS)
         cols = field[h].reshape(448, COLS)[:, q : q + 128]
         f[:, 128 * j : 128 * j + 128] = cols * scale_row[j][0:1, :]
-    lower = {}
+    stores = []
     for j in range(4):
         here = slice(128 * j, 128 * j + 128)
         inverse = inverse_factor(w[here, here])
         if j < 3:
             column = dot_nt(w[128 * (j + 1) :, here], inverse)
-            lower[j] = column
             for i in range(j + 1, 4):
                 band = column[128 * (i - j - 1) : 128 * (i - j)]
                 w[128 * i : 128 * i + 128, 128 * (j + 1) : 128 * (i + 1)] = w[
                     128 * i : 128 * i + 128, 128 * (j + 1) : 128 * (i + 1)
                 ] - dot_nt(band, column[: 128 * (i - j)])
-        x[here, here] = inverse
-        if j > 0:
-            left = jnp.concatenate([lower[k][128 * (j - k - 1) : 128 * (j - k)] for k in range(j)], axis=1)
-            x[here, : 128 * j] = -dot_nn(inverse, dot_nn(left, x[: 128 * j, : 128 * j]))
-        rotated = dot_nt(f[:, : 128 * (j + 1)], x[here, : 128 * (j + 1)])
-        for a in range(7):
-            for b in range(7):
-                r = 64 * a + 8 * b
-                out[a, b, :, here] = rotated[r : r + 7, :]
+        rotated = dot_nt(f[:, here], inverse)
+        held[:, :, :, here] = rotated.reshape(7, 8, 8, 128)
+        stores.append(
+            pltpu.make_async_copy(held.at[:, 0:7, 0:7, here], out.at[:, :, :, here], sems.at[j])
+        )
+        stores[j].start()
         if j < 3:
-            x[here, 128 * (j + 1) :] = jnp.zeros((128, 512 - 128 * (j + 1)), jnp.float32)
+            f[:, 128 * (j + 1) :] = f[:, 128 * (j + 1) :] - dot_nt(rotated, column)
+    for c in stores:
+        c.wait()
 
 
 def finish_call(packed, field, node_total):
@@ -469,11 +463,12 @@
         functools.partial(finish_kernel, node_total),
         out_shape=jax.ShapeDtypeStruct((7, 7, 7, 512), jnp.float32),
         in_specs=[pl.BlockSpec(memory_space=pltpu.VMEM)] * 2,
-        out_specs=pl.BlockSpec(memory_space=pltpu.VMEM),
+        out_specs=pl.BlockSpec(memory_space=pltpu.HBM),
         scratch_shapes=[
             pltpu.VMEM((512, 512), jnp.float32),
-            pltpu.VMEM((512, 512), jnp.float32),
             pltpu.VMEM((448, 512), jnp.float32),
+            pltpu.VMEM((7, 8, 8, 512), jnp.float32),
+            pltpu.SemaphoreType.DMA((4,)),
         ],
         compiler_params=pltpu.CompilerParams(vmem_limit_bytes=40 << 20),
     )(packed, field)

time: 91.7 us -> 90.1 us (0.983)
  Pallas kernels: 91.6 us -> 89.8 us
    pallas_call x1, Pallas kernels: 19.6 us -> 18.7 us  [finish_call(): pl.pallas_call(functools.partial(finish_kernel, node_total), out_shape=ja...]
where the time goes in v3:
time: 90.1 us; the launch traced here: 90 us
  Pallas kernels  89.8 us (100%)
    pallas_call x1, Pallas kernels, filter_call(): pl.pallas_call(filter_kernel, out_shape=(jax.ShapeDtypeStruct((PART, 7, 8...  71.1 us
    pallas_call x1, Pallas kernels, finish_call(): pl.pallas_call(functools.partial(finish_kernel, node_total), out_shape=ja...  18.7 us

profile of v3, /device:TPU:1, one launch (start us, length us, event | category | flops | bytes accessed | tf_op | source)
XLA Modules:
  0.0 90.0 jit_solution(240092915668728164)
XLA Ops:
  0.0 71.1 %shard_map.37 = (f32[2,7,8,8,256]{4,3,2,1,0:T(8,128)S(1)}, f32[160,8,128]{2,1,0:T(8,128)S(1)}) custom-call(f32[7,7,7,512]{3,2,1,0:T(8,128)} %orbitals.1, bf16[512,512]{1,0:T(8,128)(2,1)} %bitcast.2, s32[1,512]{1,0:T(1,128)} %bitcast.3), custom_call_target="tpu_custom_call" | custom-call | tf_op jit(solution)/shard_map/pallas_call | solution.py:308
  71.1 18.7 %shard_map.38 = f32[7,7,7,512]{3,2,1,0:T(8,128)} custom-call(f32[160,8,128]{2,1,0:T(8,128)S(1)} %get-tuple-element.7.packed, f32[2,7,8,8,256]{4,3,2,1,0:T(8,128)S(1)} %get-tuple-element.8.field), custom_call_target="tpu_custom_call" | custom-call | tf_op jit(solution)/shard_map/pallas_call | solution.py:462

commit v4 on v3

--- a/solution.py
+++ b/solution.py
@@ -130,7 +130,7 @@
     ]
 
 
-def filter_steps(loads, matrix, order, field, mat, ys, zs, fw, fn, ce, ssem, rsem):
+def filter_steps(finished, loads, matrix, order, field, mat, ys, zs, fw, fn, ce, ssem, rsem):
     w = lax.axis_index("wide")
     n = lax.axis_index("narrow")
     wn, wp = (w + 1) % WIDE, (w + WIDE - 1) % WIDE
@@ -249,6 +249,7 @@
         for c in copies[DEG, h]:
             c.wait_recv()
         border(DEG - 1, h)
+        finished(h)
     return pend
 
 
@@ -257,7 +258,7 @@
         {"wide": (w + a) % WIDE, "narrow": (n + b) % NARROW}
         for a in (WIDE - 1, 0, 1)
         for b in (NARROW - 1, 0, 1)
-        if (a, b) != (0, 0)
+        if a != 0
     ]
 
 
@@ -271,9 +272,11 @@
 
 
 def gram_tiles(field, tiles):
-    cols = [halves(field[h].reshape(448, COLS)) for h in range(PART)]
+    cols = []
     per = COLS // 128
-    for a in range(PART):
+
+    def finished(a):
+        cols.append(halves(field[a].reshape(448, COLS)))
         for b in range(a + 1):
             (ah, al), (bh, bl) = cols[a], cols[b]
             block = dot_tn(ah, bh) + (dot_tn(ah, bl) + dot_tn(al, bh))
@@ -283,6 +286,8 @@
                     if q <= p:
                         t = 16 * (p * (p + 1) // 2 + q)
                         tiles[t : t + 16] = block[128 * i : 128 * i + 128, 128 * j : 128 * j + 128].reshape(16, 8, 128)
+
+    return finished
 
 
 def filter_kernel(orbitals, matrix, order, field, full, tiles, held, numbers, lsem, *scratch):
@@ -297,8 +302,7 @@
     for c in loads[1:] + loads[:1]:
         c.start()
     barrier(neighbours(lax.axis_index("wide"), lax.axis_index("narrow")) + peers(*place()))
-    pend = filter_steps(loads, held, numbers, field, *scratch[:8])
-    gram_tiles(field, tiles)
+    pend = filter_steps(gram_tiles(field, tiles), loads, held, numbers, field, *scratch[:8])
     all_reduce(tiles, full, *scratch[8:])
     for c in pend:
         c.wait_send()

time: 90.1 us -> 89.5 us (level)
  no operation moved by 1% of the time
where the time goes in v4:
time: 89.5 us; the launch traced here: 89.4 us
  Pallas kernels  89.2 us (100%)
    pallas_call x1, Pallas kernels, filter_call(): pl.pallas_call(filter_kernel, out_shape=(jax.ShapeDtypeStruct((PART, 7, 8...  70.6 us
    pallas_call x1, Pallas kernels, finish_call(): pl.pallas_call(functools.partial(finish_kernel, node_total), out_shape=ja...  18.7 us

profile of v4, /device:TPU:1, one launch (start us, length us, event | category | flops | bytes accessed | tf_op | source)
XLA Modules:
  0.0 89.4 jit_solution(18317025934809491881)
XLA Ops:
  0.0 70.6 %shard_map.37 = (f32[2,7,8,8,256]{4,3,2,1,0:T(8,128)S(1)}, f32[160,8,128]{2,1,0:T(8,128)S(1)}) custom-call(f32[7,7,7,512]{3,2,1,0:T(8,128)} %orbitals.1, bf16[512,512]{1,0:T(8,128)(2,1)} %bitcast.2, s32[1,512]{1,0:T(1,128)} %bitcast.3), custom_call_target="tpu_custom_call" | custom-call | tf_op jit(solution)/shard_map/pallas_call | solution.py:312
  70.6 18.7 %shard_map.38 = f32[7,7,7,512]{3,2,1,0:T(8,128)} custom-call(f32[160,8,128]{2,1,0:T(8,128)S(1)} %get-tuple-element.7.packed, f32[2,7,8,8,256]{4,3,2,1,0:T(8,128)S(1)} %get-tuple-element.8.field), custom_call_target="tpu_custom_call" | custom-call | tf_op jit(solution)/shard_map/pallas_call | solution.py:466
